TPU v7x, 128 devices: a whole 4x4x4 slice. The times are simulated.
128 devices in a mesh: dp: 16 (over x_lo, z, core), loop: 8 (over x_hi, y).
Axes of the slice: x: 4 (x_hi: 2, x_lo: 2; x = x_hi * 2 + x_lo), y: 4, z: 4, core: 2. Of those that a mesh axis runs over, the one named last changes fastest.
Arguments:
- crop_tokens: bfloat16 [8192, 64, 1152], P(('dp', 'loop')), may hold values from -6 to 6
- crop_lengths: int32 [128, 64], P(('dp', 'loop')), may hold values from 1 to 64, 3072 in all within a row
- crop_owner: int32 [8192, 1], P(('dp', 'loop')), may hold values from 0 to 15; in each aligned block of 64 rows (0 to 63, 64 to 127, ...) at most 8 rows name the same one
- crop_slot: int32 [8192], P(('dp', 'loop')), may hold values from 0 to 31
- base_tokens: bfloat16 [4096, 32, 1152], P(('dp', 'loop')), may hold values from -1024 to 1024
- key_probe: bfloat16 [1152, 16], replicated, may hold values from -1 to 1
- value_weight: bfloat16 [1152, 1152], replicated, may hold values from -0.1875 to 0.1875
- out_weight: bfloat16 [1152, 1152], replicated, may hold values from -0.1875 to 0.1875
- text_embed: bfloat16 [4096, 1152], P(('dp', 'loop')), may hold values from -6 to 6
- pair_labels: int32 [4096], P(('dp', 'loop')), may hold values from 0 to 63
- logit_scale: float32 [1], replicated, may hold values from 2 to 8
- logit_bias: float32 [1], replicated, may hold values from -4 to -1
Outputs:
- image_embed: bfloat16 [4096, 1152], P(('dp', 'loop'))
- image_grad: float32 [4096, 1152], P(('dp', 'loop'))
- text_grad: float32 [4096, 1152], P(('dp', 'loop'))
Inputs may be any that keep to these rules, and one draw needn't show every extreme that they name: `crop_owner`: at most 8 of the crops of one device name the same owner, and in every draw the crops of some device name one owner exactly 8 times. `crop_lengths`: the lengths of one device's crops sum to 3072 and the longest is exactly 64.
All inputs are finite; a program needn't handle non-finite values.
Results may differ from a plain program's by a relative error of at most 0.01.
Values may be sent and summed in bfloat16 or wider, within the bound.
No kernel may reach another device: no remote copies, remote signals or barrier semaphores. Data moves between devices by JAX's collectives and lax.ppermute only.
A program may use at most 192 MiB of HBM per device.

v0:
```python
import math

import jax
import jax.numpy as jnp
from jax import lax
from jax.experimental import pallas as pl
from jax.experimental.pallas import tpu as pltpu
from jax.sharding import PartitionSpec as P

very_low = -1e30
norm_eps = 1e-06
highest = lax.Precision.HIGHEST
f32 = jnp.float32
bf16 = jnp.bfloat16
contract_last = (((1,), (1,)), ((), ()))
lanes = 128
sublanes = 8
col_tile = 256
token_tile = 256


def iota(shape, dim):
    return lax.broadcasted_iota(jnp.int32, shape, dim)


def head_lane(lane, heads, per_tile):
    return (lane % (heads // per_tile)) * per_tile + lane // (heads // per_tile)


def score_rows(probe_rows, tokens, head_dim):
    return lax.dot_general(
        probe_rows, tokens, contract_last, preferred_element_type=f32
    ) * (1.0 / math.sqrt(head_dim))


def softmax_rows(scores, valid, units, rounded):
    heads = scores.shape[0]
    per_tile = sublanes // units
    tiles = heads // per_tile
    row = iota(valid.shape, 0)
    lane = iota((sublanes, lanes), 1)
    peaks = jnp.zeros((sublanes, lanes), f32)
    totals = jnp.zeros((sublanes, lanes), f32)
    weights = []
    for tile in range(tiles):
        part = jnp.broadcast_to(scores[tile * per_tile : tile * per_tile + 1, :], valid.shape)
        for k in range(1, per_tile):
            head = tile * per_tile + k
            part = jnp.where(row >= k * units, scores[head : head + 1, :], part)
        masked = jnp.where(valid, part, very_low)
        peak = jnp.max(masked, axis=1, keepdims=True)
        if rounded:
            peak = peak.astype(bf16).astype(f32)
        weight = jnp.exp(masked - peak).astype(bf16).astype(f32)
        amount = jnp.sum(weight, axis=1, keepdims=True)
        peaks = jnp.where(lane == tile, peak, peaks)
        totals = jnp.where(lane == tile, amount, totals)
        weights.append(weight)
    row = iota((sublanes, lanes), 0)
    for k in range(1, per_tile):
        peaks = jnp.where(row >= k * units, jnp.roll(peaks, k * tiles, axis=1), peaks)
        totals = jnp.where(row >= k * units, jnp.roll(totals, k * tiles, axis=1), totals)
    return jnp.concatenate(weights, axis=0).astype(bf16), peaks, totals


def mix_rows(rows_ref, stride, step, weights, tokens):
    mixed = [
        jnp.dot(weight, token, preferred_element_type=f32)
        for weight, token in zip(weights, tokens)
    ]
    height = len(mixed) * sublanes
    for tile in range(mixed[0].shape[0] // sublanes):
        start = tile * stride + step * height
        if not isinstance(start, int):
            start = pl.multiple_of(start, height)
        rows_ref[pl.ds(start, height), :] = jnp.concatenate(
            [part[tile * sublanes : (tile + 1) * sublanes, :] for part in mixed], axis=0
        ).astype(bf16)


def project_tile(rows_ref, value_ref, stride, low, high, head_dim, units):
    span = sublanes // units * head_dim
    first = low // span
    last = (high - 1) // span
    stacked = jnp.dot(
        rows_ref[first * stride : (last + 1) * stride, :],
        value_ref[:, low:high],
        preferred_element_type=f32,
    ).reshape(last + 1 - first, stride // sublanes, sublanes, high - low)
    shape = (1, sublanes, high - low)
    kind = iota(shape, 1) // units
    column = iota(shape, 2) + low - kind * head_dim
    total = jnp.where(column >= first * span, stacked[0], 0.0)
    for tile in range(first + 1, last + 1):
        total = jnp.where(column >= tile * span, stacked[tile - first], total)
    if units < sublanes:
        owner = (column >= 0) & (column % span < head_dim)
        total = jnp.where(owner, total, 0.0)
    return total.reshape(stride, high - low)


def project_heads(rows_ref, value_ref, stride, model, head_dim, units, finish):
    waiting = None
    for low in range(0, model, col_tile):
        high = min(low + col_tile, model)
        current = project_tile(rows_ref, value_ref, stride, low, high, head_dim, units)
        if waiting is not None:
            finish(*waiting)
        waiting = (low, high, current)
    finish(*waiting)


def column_of(row):
    square = (row.shape[1], row.shape[1])
    return jnp.sum(jnp.where(iota(square, 0) == iota(square, 1), row, 0), axis=1, keepdims=True)


def crop_kernel(
    token_hbm,
    probe_ref,
    length_ref,
    owner_ref,
    slot_ref,
    value_hbm,
    send_ref,
    token_ref,
    rows_ref,
    meta_ref,
    limit_ref,
    member_ref,
    value_ref,
    token_sem,
    value_sem,
    *,
    capacity,
):
    crops, width, model = token_ref.shape
    heads = probe_ref.shape[0]
    head_dim = model // heads
    slots = send_ref.shape[0]
    units = token_tile // width
    per_tile = sublanes // units
    rows = crops * per_tile
    blocks = token_sem.shape[0]
    per_step = crops // blocks
    parts = per_step // units

    def token_copy(step):
        where = pl.ds(step * per_step, per_step)
        return pltpu.make_async_copy(token_hbm.at[where], token_ref.at[where], token_sem.at[step])

    for step in range(blocks):
        token_copy(step).start()
    value_copy = pltpu.make_async_copy(value_hbm, value_ref, value_sem)
    value_copy.start()
    expand = (rows, crops)
    owner_of = iota(expand, 0) // sublanes * units + iota(expand, 0) % units
    chosen = owner_of == iota(expand, 1)
    limit_ref[...] = jnp.broadcast_to(
        jnp.sum(jnp.where(chosen, length_ref[...], 0), axis=1, keepdims=True), limit_ref.shape
    )
    wide = (sublanes, token_tile)
    offset = iota(wide, 1) - iota(wide, 0) % units * width

    def tokens_of(step, part):
        start = step * per_step + part * units
        return token_ref[pl.ds(start, units)].reshape(units * width, model)

    owner_row = owner_ref[...]
    square = (crops, crops)
    earlier = (column_of(owner_row) == owner_row) & (iota(square, 0) < iota(square, 1))
    rank = jnp.sum(earlier.astype(jnp.int32), axis=0, keepdims=True)
    place = owner_row * capacity + rank
    turned = (crops, rows)
    place_row = jnp.sum(
        jnp.where(
            iota(turned, 1) // sublanes * units + iota(turned, 1) % units == iota(turned, 0),
            column_of(place),
            0,
        ),
        axis=0,
        keepdims=True,
    )
    member_ref[...] = (iota((slots, rows), 0) == place_row).astype(bf16)
    slot_of = jnp.sum(jnp.where(chosen, slot_ref[...], 0), axis=1, keepdims=True)
    lane = iota((rows, lanes), 1)
    lead = iota((rows, lanes), 0) % sublanes < units
    extra = jnp.where(lane == 3 * heads, slot_of.astype(f32), 0.0) + jnp.where(
        lane == 3 * heads + 1, 1.0, 0.0
    )
    meta_ref[...] = jnp.where(lead, extra, 0.0)

    def scores_of(step):
        return tuple(
            score_rows(probe_ref[...], tokens_of(step, part), head_dim) for part in range(parts)
        )

    def weigh(step, scores):
        weights = []
        for part in range(parts):
            start = pl.multiple_of((step * parts + part) * sublanes, sublanes)
            limit = jnp.concatenate(
                [limit_ref[pl.ds(start, sublanes), :]] * (token_tile // lanes), axis=1
            )
            weight, peaks, totals = softmax_rows(
                scores[part], (offset >= 0) & (offset < limit), units, True
            )
            coarse = totals.astype(bf16).astype(f32)
            meta_ref[pl.ds(start, sublanes), :] += (
                peaks
                + jnp.roll(coarse, heads, axis=1)
                + jnp.roll(totals - coarse, 2 * heads, axis=1)
            )
            weights.append(weight)
        return tuple(weights)

    def mix(step, weights):
        mix_rows(
            rows_ref, rows, step, weights, [tokens_of(step, part) for part in range(parts)]
        )

    token_copy(0).wait()
    scores = scores_of(0)
    token_copy(1).wait()
    following = scores_of(1)
    weights = weigh(0, scores)

    def advance(step, carry):
        scores, weights = carry
        token_copy(step + 1).wait()
        mix(step - 1, weights)
        following = scores_of(step + 1)
        return following, weigh(step, scores)

    scores, weights = lax.fori_loop(1, blocks - 1, advance, (following, weights))
    mix(blocks - 2, weights)
    mix(blocks - 1, weigh(blocks - 1, scores))
    send_ref[:, model:] = jnp.dot(
        member_ref[...], meta_ref[...].astype(bf16), preferred_element_type=f32
    ).astype(bf16)
    value_copy.wait()

    def finish(low, high, summed):
        send_ref[:, low:high] = jnp.dot(
            member_ref[...], summed.astype(bf16), preferred_element_type=f32
        ).astype(bf16)

    project_heads(rows_ref, value_ref, rows, model, head_dim, units, finish)


def base_kernel(
    token_hbm,
    probe_ref,
    value_hbm,
    sum_ref,
    peak_ref,
    total_ref,
    token_ref,
    rows_ref,
    value_ref,
    token_sem,
    value_sem,
    *,
    per_tile,
):
    count, width, model = token_ref.shape
    heads = probe_ref.shape[0]
    head_dim = model // heads
    units = token_tile // width
    blocks = count // units
    copies = []
    for block in range(blocks):
        where = pl.ds(block * units, units)
        copies.append(
            pltpu.make_async_copy(token_hbm.at[where], token_ref.at[where], token_sem.at[block])
        )
        copies[-1].start()
    value_copy = pltpu.make_async_copy(value_hbm, value_ref, value_sem)
    value_copy.start()
    wide = (sublanes, token_tile)
    offset = iota(wide, 1) - iota(wide, 0) * width
    valid = (offset >= 0) & (offset < width)
    lane = iota((lanes, lanes), 1)
    order = (head_lane(lane, heads, per_tile) == iota((lanes, lanes), 0)) & (lane < heads)
    stats = []
    weights = []
    tokens = []
    for block in range(blocks):
        copies[block].wait()
        tokens.append(
            token_ref[block * units : (block + 1) * units].reshape(units * width, model)
        )
        scores = score_rows(probe_ref[...], tokens[block], head_dim)
        weight, peaks, totals = softmax_rows(scores, valid, units, False)
        weights.append(weight)
        stats.append((peaks, totals))
        if block % 2 == 1:
            pair = slice(block - 1, block + 1)
            mix_rows(rows_ref, count, block // 2, weights[pair], tokens[pair])
    for index, out_ref in ((0, peak_ref), (1, total_ref)):
        out_ref[...] = jnp.dot(
            jnp.concatenate([pair[index] for pair in stats], axis=0),
            order.astype(f32),
            preferred_element_type=f32,
            precision=highest,
        )
    value_copy.wait()

    def finish(low, high, summed):
        sum_ref[:, low:high] = summed

    project_heads(rows_ref, value_ref, count, model, head_dim, units, finish)


def two_part_dot(matrix, table):
    coarse = matrix.astype(bf16)
    fine = (matrix - coarse.astype(f32)).astype(bf16)
    return jnp.dot(coarse, table, preferred_element_type=f32) + jnp.dot(
        fine, table, preferred_element_type=f32
    )


def merge_kernel(
    arrived_ref,
    base_ref,
    base_peak_ref,
    base_total_ref,
    text_ref,
    label_ref,
    out_weight_ref,
    embed_ref,
    own_ref,
    peak_ref,
    *,
    heads,
    per_tile,
):
    count, model = base_ref.shape
    head_dim = model // heads
    slots = arrived_ref.shape[0]
    meta = arrived_ref[:, model:].astype(f32)
    slot_column = jnp.where(
        meta[:, 3 * heads + 1 : 3 * heads + 2] > 0.5, meta[:, 3 * heads : 3 * heads + 1], -1.0
    )
    slot_wide = jnp.broadcast_to(slot_column, (slots, lanes))
    for image in range(count):
        peak_ref[image : image + 1, :] = jnp.max(
            jnp.where(slot_wide == float(image), meta, very_low), axis=0, keepdims=True
        )
    base_peak = base_peak_ref[...]
    joint = jnp.maximum(peak_ref[...], base_peak)
    member = (slot_column == iota((slots, count), 1).astype(f32)).astype(f32)
    joint_at = jnp.dot(member, joint, preferred_element_type=f32, precision=highest)
    used = (iota((slots, lanes), 1) < heads) & (slot_wide >= 0.0)
    rescale = jnp.where(used, jnp.exp(jnp.where(used, meta - joint_at, 0.0)), 0.0).astype(bf16)
    totals = jnp.roll(meta, -heads, axis=1) + jnp.roll(meta, -2 * heads, axis=1)
    lane = iota((count, lanes), 1)
    base_rescale = jnp.where(lane < heads, jnp.exp(base_peak - joint), 0.0)
    collected = lax.dot_general(
        member,
        totals * rescale.astype(f32),
        (((0,), (0,)), ((), ())),
        preferred_element_type=f32,
        precision=highest,
    )
    inverse = 1.0 / (collected + base_total_ref[...] * base_rescale + jnp.where(lane < heads, 0.0, 1.0))
    table_shape = (lanes, model)
    table_row = iota(table_shape, 0)
    column = iota(table_shape, 1) - head_lane(table_row, heads, per_tile) * head_dim
    table = ((column >= 0) & (column < head_dim) & (table_row < heads)).astype(bf16)
    scaled = arrived_ref[:, :model].astype(f32) * jnp.dot(
        rescale, table, preferred_element_type=f32
    )
    crop_sum = lax.dot_general(
        member.astype(bf16),
        scaled.astype(bf16),
        (((0,), (0,)), ((), ())),
        preferred_element_type=f32,
    )
    factors = two_part_dot(jnp.concatenate([inverse, base_rescale * inverse], axis=0), table)
    pooled = (crop_sum * factors[:count] + base_ref[...] * factors[count:]).astype(bf16)
    text = text_ref[...].astype(f32)
    text_unit = (
        text * lax.rsqrt(jnp.sum(text * text, axis=1, keepdims=True) + norm_eps)
    ).astype(bf16)
    double = 2 * count
    for part in range(model // lanes):
        own_ref[part * double + count : (part + 1) * double, :] = text_unit[
            :, part * lanes : (part + 1) * lanes
        ]
    own_ref[model // lanes * double :, :] = jnp.broadcast_to(
        jnp.concatenate([label_ref[...].astype(f32)] * (lanes // count), axis=1),
        (own_ref.shape[0] - model // lanes * double, lanes),
    ).astype(bf16)
    features = jnp.dot(pooled, out_weight_ref[...], preferred_element_type=f32)
    embed_ref[...] = features.astype(bf16)
    image_unit = (
        features * lax.rsqrt(jnp.sum(features * features, axis=1, keepdims=True) + norm_eps)
    ).astype(bf16)
    for part in range(model // lanes):
        own_ref[part * double : part * double + count, :] = image_unit[
            :, part * lanes : (part + 1) * lanes
        ]


def grad_kernel(scale_ref, bias_ref, label_ref, *refs):
    pieces, (image_grad_ref, text_grad_ref, everyone) = refs[:-3], refs[-3:]
    count, model = image_grad_ref.shape
    double = 2 * count
    parts = model // lanes
    label_rows = []
    for index, piece in enumerate(pieces):
        for part in range(parts):
            everyone[
                index * double : (index + 1) * double, part * lanes : (part + 1) * lanes
            ] = piece[part * double : (part + 1) * double, :]
        label_rows.append(piece[parts * double :, :].astype(f32)[:1])
    lane = iota((1, lanes), 1)
    per_row = lanes // double
    label_row = []
    for first in range(0, len(pieces), per_row):
        row = label_rows[first]
        for k in range(1, per_row):
            row = jnp.where(lane >= k * double, label_rows[first + k], row)
        label_row.append(row)
    label_row = jnp.concatenate(label_row, axis=1)
    label_column = column_of(label_ref[...]).astype(f32)
    label_column = jnp.concatenate([label_column, label_column], axis=0)
    scale = scale_ref[0]
    bias = bias_ref[0]
    sign = jnp.where(label_column == label_row, 1.0, -1.0)
    logits = scale * lax.dot_general(
        everyone[:double, :], everyone[...], contract_last, preferred_element_type=f32
    ) + bias
    tile = scale * (-sign * jax.nn.sigmoid(-sign * logits))
    other_side = (iota(tile.shape, 1) % double >= count) == (iota(tile.shape, 0) < count)
    tile = jnp.where(other_side, tile, 0.0).astype(bf16)
    grads = jnp.dot(tile, everyone[...], preferred_element_type=f32)
    image_grad_ref[...] = grads[:count]
    text_grad_ref[...] = grads[count:]


def per_device(
    crop_tokens,
    crop_lengths,
    crop_owner,
    crop_slot,
    base_tokens,
    key_probe,
    value_weight,
    out_weight,
    text_embed,
    pair_labels,
    logit_scale,
    logit_bias,
):
    owners = lax.axis_size("dp")
    peers = lax.axis_size("loop")
    crops, width, model = crop_tokens.shape
    count, base_width, _ = base_tokens.shape
    heads = key_probe.shape[1]
    capacity = max(2, (2 * crops + owners - 1) // owners)
    slots = owners * capacity
    padded = model + lanes
    blocks = 8
    per_tile = sublanes * width // token_tile
    rows = crops * per_tile
    payload = (model // lanes * 2 * count + 16, lanes)
    vmem = pl.BlockSpec(memory_space=pltpu.VMEM)
    smem = pl.BlockSpec(memory_space=pltpu.SMEM)
    anywhere = pl.BlockSpec(memory_space=pl.ANY)
    probe_rows = key_probe.T

    def crop_body(*refs):
        crop_kernel(*refs, capacity=capacity)

    def base_body(*refs):
        base_kernel(*refs, per_tile=per_tile)

    def merge_body(*refs):
        merge_kernel(*refs, heads=heads, per_tile=per_tile)

    send = pl.pallas_call(
        crop_body,
        in_specs=[anywhere, vmem, vmem, vmem, vmem, anywhere],
        out_specs=vmem,
        scratch_shapes=[
            pltpu.VMEM((crops, width, model), bf16),
            pltpu.VMEM((crops * heads, model), bf16),
            pltpu.VMEM((rows, lanes), f32),
            pltpu.VMEM((rows, lanes), jnp.int32),
            pltpu.VMEM((slots, rows), bf16),
            pltpu.VMEM((model, model), bf16),
            pltpu.SemaphoreType.DMA((blocks,)),
            pltpu.SemaphoreType.DMA,
        ],
        out_shape=jax.ShapeDtypeStruct((slots, padded), bf16),
        name="crop_partial",
    )(
        crop_tokens,
        probe_rows,
        crop_lengths,
        crop_owner.reshape(1, crops),
        crop_slot.reshape(1, crops),
        value_weight,
    )
    arrived = lax.all_to_all(send, "dp", split_axis=0, concat_axis=0, tiled=True)
    arrived = pltpu.with_memory_space_constraint(arrived, pltpu.VMEM)
    base_sum, base_peak, base_total = pl.pallas_call(
        base_body,
        in_specs=[anywhere, vmem, anywhere],
        out_specs=[vmem] * 3,
        out_shape=[
            jax.ShapeDtypeStruct((count, model), f32),
            jax.ShapeDtypeStruct((count, lanes), f32),
            jax.ShapeDtypeStruct((count, lanes), f32),
        ],
        scratch_shapes=[
            pltpu.VMEM((count, base_width, model), bf16),
            pltpu.VMEM((count * heads, model), bf16),
            pltpu.VMEM((model, model), bf16),
            pltpu.SemaphoreType.DMA((count * base_width // token_tile,)),
            pltpu.SemaphoreType.DMA,
        ],
        name="base_partial",
    )(base_tokens, probe_rows, value_weight)
    label_row = pair_labels.reshape(1, count)
    image_embed, own = pl.pallas_call(
        merge_body,
        in_specs=[vmem] * 7,
        out_specs=[vmem] * 2,
        out_shape=[
            jax.ShapeDtypeStruct((count, model), bf16),
            jax.ShapeDtypeStruct(payload, bf16),
        ],
        scratch_shapes=[pltpu.VMEM((count, lanes), f32)],
        name="merge_parts",
    )(
        arrived,
        base_sum,
        base_peak,
        base_total,
        text_embed,
        label_row,
        pltpu.with_memory_space_constraint(out_weight, pltpu.VMEM),
    )

    def peer_copy(array, half, turn):
        column = peers // 2
        pairs = [
            (p, (p // column ^ half) * column + (p % column + turn) % column) for p in range(peers)
        ]
        return lax.ppermute(array, "loop", pairs)

    other = peer_copy(own, 1, 0)
    across = peer_copy(own, 0, 2)
    after = peer_copy(own, 0, 1)
    before = peer_copy(own, 0, 3)
    received = [
        other,
        after,
        before,
        across,
        peer_copy(other, 0, 1),
        peer_copy(other, 0, 3),
        peer_copy(across, 1, 0),
    ]
    pieces = [own] + [pltpu.with_memory_space_constraint(piece, pltpu.VMEM) for piece in received]
    image_grad, text_grad = pl.pallas_call(
        grad_kernel,
        in_specs=[smem, smem, vmem] + [vmem] * peers,
        out_specs=[vmem] * 2,
        out_shape=[
            jax.ShapeDtypeStruct((count, model), f32),
            jax.ShapeDtypeStruct((count, model), f32),
        ],
        scratch_shapes=[pltpu.VMEM((peers * 2 * count, model), bf16)],
        name="loss_grads",
    )(logit_scale, logit_bias, label_row, *pieces)
    return (image_embed, image_grad, text_grad)


def solution(mesh):
    return jax.shard_map(
        per_device,
        mesh=mesh,
        in_specs=(
            P(("dp", "loop"), None, None),
            P(("dp", "loop"), None),
            P(("dp", "loop"), None),
            P(("dp", "loop")),
            P(("dp", "loop"), None, None),
            P(),
            P(),
            P(),
            P(("dp", "loop"), None),
            P(("dp", "loop")),
            P(),
            P(),
        ),
        out_specs=(P(("dp", "loop"), None), P(("dp", "loop"), None), P(("dp", "loop"), None)),
        check_vma=False,
    )
```

profile of v0, /device:TPU:0, one launch (start us, length us, event | category | flops | bytes accessed | tf_op | source)
XLA Modules:
  0.0 51.8 jit_solution(3110068723325278216)
XLA Ops:
  0.6 9.5 %crop_partial.1 = bf16[128,1280]{1,0:T(8,128)(2,1)} custom-call(bf16[64,64,1152]{2,1,0:T(8,128)(2,1)} %refs_0_.2, bf16[16,1152]{1,0:T(8,128)(2,1)} %bitcast.8, s32[1,64]{1,0:T(1,128)} %refs_2_.2, s32[1,64]{1,0:T(1,128)} %bitcast.12, s32[1,64]{1,0:T(1,128)} %bitcast.13, bf16[1152,1152]{1,0:T(8,128)(2,1)} %refs_2_.3), custom_call_target="tpu_custom_call" | custom-call | tf_op jit(solution)/shard_map/crop_partial/pallas_call | solution.py:483
  10.1 6.5 %all-to-all-start = ((bf16[16,8,1280]{2,1,0:T(8,128)(2,1)}), bf16[16,8,1280]{2,1,0:T(8,128)(2,1)S(1)}, u32[]{:S(2)}, u32[]{:S(2)}) async-start(bf16[16,8,1280]{2,1,0:T(8,128)(2,1)} %bitcast.7), calls=%async_computation | async-start | bytes 655360 | tf_op jit(solution)/shard_map/all_to_all | solution.py:507
  16.6 0.0 copy-start
  16.6 6.1 %base_partial.1 = (f32[32,1152]{1,0:T(8,128)}, f32[32,128]{1,0:T(8,128)}, f32[32,128]{1,0:T(8,128)}) custom-call(bf16[32,32,1152]{2,1,0:T(8,128)(2,1)} %refs_0_.3, bf16[16,1152]{1,0:T(8,128)(2,1)} %bitcast.9, bf16[1152,1152]{1,0:T(8,128)(2,1)} %refs_2_.3), custom_call_target="tpu_custom_call" | custom-call | tf_op jit(solution)/shard_map/base_partial/pallas_call | solution.py:509
  22.7 2.6 %all-to-all-done = bf16[16,8,1280]{2,1,0:T(8,128)(2,1)S(1)} async-done(((bf16[16,8,1280]{2,1,0:T(8,128)(2,1)}), bf16[16,8,1280]{2,1,0:T(8,128)(2,1)S(1)}, u32[]{:S(2)}, u32[]{:S(2)}) %all-to-all-start) | async-done | bytes 327712 | tf_op jit(solution)/shard_map/all_to_all | solution.py:507
  25.3 0.0 copy-done
  25.3 3.3 %merge_parts.1 = (bf16[32,1152]{1,0:T(8,128)(2,1)}, bf16[592,128]{1,0:T(8,128)(2,1)}) custom-call(bf16[128,1280]{1,0:T(8,128)(2,1)S(1)} %bitcast.6, f32[32,1152]{1,0:T(8,128)} %get-tuple-element.10.refs_1_, f32[32,128]{1,0:T(8,128)} %get-tuple-element.11.refs_2_, f32[32,128]{1,0:T(8,128)} %get-tuple-element.12.refs_3_, bf16[32,1152]{1,0:T(8,128)(2,1)} %refs_4_.1, ...), custom_call_target="tpu_custom_call" | custom-call | tf_op jit(solution)/shard_map/merge_parts/pallas_call | solution.py:528
  28.6 3.2 %collective-permute-start.3 = (bf16[592,128]{1,0:T(8,128)(2,1)}, bf16[592,128]{1,0:T(8,128)(2,1)S(1)}, u32[]{:S(2)}, u32[]{:S(2)}) collective-permute-start(bf16[592,128]{1,0:T(8,128)(2,1)} %get-tuple-element.14.refs_0_), channel_id=1, source_target_pairs={{0,2},{1,3},{2,0},{3,1},{4,6},{5,7},{6,4},{7,5},{8,10},{9,11},{10,... | collective-permute-start | bytes 454664 | tf_op jit(solution)/shard_map/ppermute | solution.py:553
  31.8 2.7 %collective-permute-start = (bf16[592,128]{1,0:T(8,128)(2,1)}, bf16[592,128]{1,0:T(8,128)(2,1)S(1)}, u32[]{:S(2)}, u32[]{:S(2)}) collective-permute-start(bf16[592,128]{1,0:T(8,128)(2,1)} %get-tuple-element.14.refs_0_), channel_id=1, source_target_pairs={{0,4},{1,5},{2,6},{3,7},{4,0},{5,1},{6,2},{7,3},{8,12},{9,13},{10,... | collective-permute-start | bytes 454664 | tf_op jit(solution)/shard_map/ppermute | solution.py:553
  34.6 1.1 %collective-permute-start.2 = (bf16[592,128]{1,0:T(8,128)(2,1)}, bf16[592,128]{1,0:T(8,128)(2,1)S(1)}, u32[]{:S(2)}, u32[]{:S(2)}) collective-permute-start(bf16[592,128]{1,0:T(8,128)(2,1)} %get-tuple-element.14.refs_0_), channel_id=1, source_target_pairs={{0,3},{1,0},{2,1},{3,2},{4,7},{5,4},{6,5},{7,6},{8,11},{9,8},{10,9... | collective-permute-start | bytes 454664 | tf_op jit(solution)/shard_map/ppermute | solution.py:553
  35.6 1.0 %collective-permute-start.1 = (bf16[592,128]{1,0:T(8,128)(2,1)}, bf16[592,128]{1,0:T(8,128)(2,1)S(1)}, u32[]{:S(2)}, u32[]{:S(2)}) collective-permute-start(bf16[592,128]{1,0:T(8,128)(2,1)} %get-tuple-element.14.refs_0_), channel_id=1, source_target_pairs={{0,1},{1,2},{2,3},{3,0},{4,5},{5,6},{6,7},{7,4},{8,9},{9,10},{10,1... | collective-permute-start | bytes 454664 | tf_op jit(solution)/shard_map/ppermute | solution.py:553
  36.6 0.0 collective-permute-done.3.refs_4_
  36.6 2.3 %collective-permute-start.6 = (bf16[592,128]{1,0:T(8,128)(2,1)S(1)}, bf16[592,128]{1,0:T(8,128)(2,1)S(1)}, u32[]{:S(2)}, u32[]{:S(2)}) collective-permute-start(bf16[592,128]{1,0:T(8,128)(2,1)S(1)} %collective-permute-done.3.refs_4_), channel_id=1, source_target_pairs={{0,4},{1,5},{2,6},{3,7},{4,0},{5,1},{6,2},{7,3},{8,12},{9,13},{10,... | collective-permute-start | bytes 454664 | tf_op jit(solution)/shard_map/ppermute | solution.py:553
  38.9 0.0 collective-permute-done.refs_1_
  38.9 4.0 %collective-permute-start.5 = (bf16[592,128]{1,0:T(8,128)(2,1)S(1)}, bf16[592,128]{1,0:T(8,128)(2,1)S(1)}, u32[]{:S(2)}, u32[]{:S(2)}) collective-permute-start(bf16[592,128]{1,0:T(8,128)(2,1)S(1)} %collective-permute-done.refs_1_), channel_id=1, source_target_pairs={{0,3},{1,0},{2,1},{3,2},{4,7},{5,4},{6,5},{7,6},{8,11},{9,8},{10,9... | collective-permute-start | bytes 454664 | tf_op jit(solution)/shard_map/ppermute | solution.py:553
  42.9 0.0 collective-permute-start.4
  44.2 0.0 collective-permute-done.2.refs_3_
  44.2 0.0 collective-permute-done.1.refs_2_
  44.2 0.0 collective-permute-done.6.refs_7_
  44.3 1.4 %collective-permute-done.5.refs_6_ = bf16[592,128]{1,0:T(8,128)(2,1)S(1)} collective-permute-done((bf16[592,128]{1,0:T(8,128)(2,1)S(1)}, bf16[592,128]{1,0:T(8,128)(2,1)S(1)}, u32[]{:S(2)}, u32[]{:S(2)}) %collective-permute-start.5) | collective-permute-done | bytes 151584 | tf_op jit(solution)/shard_map/ppermute | solution.py:553
  45.6 3.7 %collective-permute-done.4.refs_5_ = bf16[592,128]{1,0:T(8,128)(2,1)S(1)} collective-permute-done((bf16[592,128]{1,0:T(8,128)(2,1)S(1)}, bf16[592,128]{1,0:T(8,128)(2,1)S(1)}, u32[]{:S(2)}, u32[]{:S(2)}) %collective-permute-start.4) | collective-permute-done | bytes 151584 | tf_op jit(solution)/shard_map/ppermute | solution.py:553
  49.3 2.5 %loss_grads.1 = (f32[32,1152]{1,0:T(8,128)}, f32[32,1152]{1,0:T(8,128)}) custom-call(f32[1]{0:T(128)S(6)} %copy.15.scale_ref, f32[1]{0:T(128)S(6)} %copy.16.bias_ref, s32[1,32]{1,0:T(1,128)} %bitcast.11, bf16[592,128]{1,0:T(8,128)(2,1)} %get-tuple-element.14.refs_0_, bf16[592,128]{1,0:T(8,128)(2,1)S(1)} %collective-permute-done.refs_1_, ...), custom_call_target="tpu_custom_call" | custom-call | tf_op jit(solution)/shard_map/loss_grads/pallas_call | solution.py:569
Async XLA Ops:
  10.1 15.2 %all-to-all-start = ((bf16[16,8,1280]{2,1,0:T(8,128)(2,1)}), bf16[16,8,1280]{2,1,0:T(8,128)(2,1)S(1)}, u32[]{:S(2)}, u32[]{:S(2)}) async-start(bf16[16,8,1280]{2,1,0:T(8,128)(2,1)} %bitcast.7), calls=%async_computation | async-start | bytes 655360 | tf_op jit(solution)/shard_map/all_to_all | solution.py:507
  16.6 8.7 %copy-start = (bf16[1152,1152]{1,0:T(8,128)(2,1)S(1)}, bf16[1152,1152]{1,0:T(8,128)(2,1)}, u32[]{:S(2)}) copy-start(bf16[1152,1152]{1,0:T(8,128)(2,1)} %refs_6_.1) | copy-start | bytes 7962628
  28.6 8.0 %collective-permute-start.3 = (bf16[592,128]{1,0:T(8,128)(2,1)}, bf16[592,128]{1,0:T(8,128)(2,1)S(1)}, u32[]{:S(2)}, u32[]{:S(2)}) collective-permute-start(bf16[592,128]{1,0:T(8,128)(2,1)} %get-tuple-element.14.refs_0_), channel_id=1, source_target_pairs={{0,2},{1,3},{2,0},{3,1},{4,6},{5,7},{6,4},{7,5},{8,10},{9,11},{10,... | collective-permute-start | bytes 454664 | tf_op jit(solution)/shard_map/ppermute | solution.py:553
  31.8 7.0 %collective-permute-start = (bf16[592,128]{1,0:T(8,128)(2,1)}, bf16[592,128]{1,0:T(8,128)(2,1)S(1)}, u32[]{:S(2)}, u32[]{:S(2)}) collective-permute-start(bf16[592,128]{1,0:T(8,128)(2,1)} %get-tuple-element.14.refs_0_), channel_id=1, source_target_pairs={{0,4},{1,5},{2,6},{3,7},{4,0},{5,1},{6,2},{7,3},{8,12},{9,13},{10,... | collective-permute-start | bytes 454664 | tf_op jit(solution)/shard_map/ppermute | solution.py:553
  34.6 9.6 %collective-permute-start.2 = (bf16[592,128]{1,0:T(8,128)(2,1)}, bf16[592,128]{1,0:T(8,128)(2,1)S(1)}, u32[]{:S(2)}, u32[]{:S(2)}) collective-permute-start(bf16[592,128]{1,0:T(8,128)(2,1)} %get-tuple-element.14.refs_0_), channel_id=1, source_target_pairs={{0,3},{1,0},{2,1},{3,2},{4,7},{5,4},{6,5},{7,6},{8,11},{9,8},{10,9... | collective-permute-start | bytes 454664 | tf_op jit(solution)/shard_map/ppermute | solution.py:553
  35.6 8.6 %collective-permute-start.1 = (bf16[592,128]{1,0:T(8,128)(2,1)}, bf16[592,128]{1,0:T(8,128)(2,1)S(1)}, u32[]{:S(2)}, u32[]{:S(2)}) collective-permute-start(bf16[592,128]{1,0:T(8,128)(2,1)} %get-tuple-element.14.refs_0_), channel_id=1, source_target_pairs={{0,1},{1,2},{2,3},{3,0},{4,5},{5,6},{6,7},{7,4},{8,9},{9,10},{10,1... | collective-permute-start | bytes 454664 | tf_op jit(solution)/shard_map/ppermute | solution.py:553
  36.6 7.6 %collective-permute-start.6 = (bf16[592,128]{1,0:T(8,128)(2,1)S(1)}, bf16[592,128]{1,0:T(8,128)(2,1)S(1)}, u32[]{:S(2)}, u32[]{:S(2)}) collective-permute-start(bf16[592,128]{1,0:T(8,128)(2,1)S(1)} %collective-permute-done.3.refs_4_), channel_id=1, source_target_pairs={{0,4},{1,5},{2,6},{3,7},{4,0},{5,1},{6,2},{7,3},{8,12},{9,13},{10,... | collective-permute-start | bytes 454664 | tf_op jit(solution)/shard_map/ppermute | solution.py:553
  38.9 6.8 %collective-permute-start.5 = (bf16[592,128]{1,0:T(8,128)(2,1)S(1)}, bf16[592,128]{1,0:T(8,128)(2,1)S(1)}, u32[]{:S(2)}, u32[]{:S(2)}) collective-permute-start(bf16[592,128]{1,0:T(8,128)(2,1)S(1)} %collective-permute-done.refs_1_), channel_id=1, source_target_pairs={{0,3},{1,0},{2,1},{3,2},{4,7},{5,4},{6,5},{7,6},{8,11},{9,8},{10,9... | collective-permute-start | bytes 454664 | tf_op jit(solution)/shard_map/ppermute | solution.py:553
  42.9 6.4 %collective-permute-start.4 = (bf16[592,128]{1,0:T(8,128)(2,1)S(1)}, bf16[592,128]{1,0:T(8,128)(2,1)S(1)}, u32[]{:S(2)}, u32[]{:S(2)}) collective-permute-start(bf16[592,128]{1,0:T(8,128)(2,1)S(1)} %collective-permute-done.refs_1_), channel_id=1, source_target_pairs={{0,1},{1,2},{2,3},{3,0},{4,5},{5,6},{6,7},{7,4},{8,9},{9,10},{10,1... | collective-permute-start | bytes 454664 | tf_op jit(solution)/shard_map/ppermute | solution.py:553
where the time goes:
time: 52.1 us; the launch traced here: 51.8 us
  Pallas kernels  21.4 us (41%)
  starting transfers between devices  20.7 us (40%)
  waiting for transfers between devices  7.67 us (15%)
  between operations  1.99 us (4%)
    ppermute x7, starting transfers between devices, peer_copy(): return lax.ppermute(array, 'loop', pairs)  14.3 us
    pallas_call x1, Pallas kernels, per_device(): pl.pallas_call(crop_body, in_specs=[anywhere, vmem, vmem, vmem, vmem, any...  9.5 us
    all_to_all x1, starting transfers between devices, per_device(): lax.all_to_all(send, 'dp', split_axis=0, concat_axis=0, tiled=True)  6.46 us
    pallas_call x1, Pallas kernels, per_device(): pl.pallas_call(base_body, in_specs=[anywhere, vmem, anywhere], out_specs=...  6.1 us
    ppermute x7, waiting for transfers between devices, peer_copy(): return lax.ppermute(array, 'loop', pairs)  5.08 us
    pallas_call x1, Pallas kernels, per_device(): pl.pallas_call(merge_body, in_specs=[vmem] * 7, out_specs=[vmem] * 2, out...  3.31 us
    all_to_all x1, waiting for transfers between devices, per_device(): lax.all_to_all(send, 'dp', split_axis=0, concat_axis=0, tiled=True)  2.6 us
    pallas_call x1, Pallas kernels, per_device(): pl.pallas_call(grad_kernel, in_specs=[smem, smem, vmem] + [vmem] * peers,...  2.47 us
  transfers between devices with their start and end apart: 8, of which 3 were waited for; matrix products, arithmetic and copies ran while one was open for 0% of the time, Pallas kernels for 12%

commit v1 on v0

--- a/solution.py
+++ b/solution.py
@@ -511,9 +511,9 @@
         in_specs=[anywhere, vmem, anywhere],
         out_specs=[vmem] * 3,
         out_shape=[
-            jax.ShapeDtypeStruct((count, model), f32),
-            jax.ShapeDtypeStruct((count, lanes), f32),
-            jax.ShapeDtypeStruct((count, lanes), f32),
+            pltpu.VMEM((count, model), f32),
+            pltpu.VMEM((count, lanes), f32),
+            pltpu.VMEM((count, lanes), f32),
         ],
         scratch_shapes=[
             pltpu.VMEM((count, base_width, model), bf16),
@@ -524,23 +524,23 @@
         ],
         name="base_partial",
     )(base_tokens, probe_rows, value_weight)
-    label_row = pair_labels.reshape(1, count)
+    label_row = pltpu.with_memory_space_constraint(pair_labels.reshape(1, count), pltpu.VMEM)
     image_embed, own = pl.pallas_call(
         merge_body,
         in_specs=[vmem] * 7,
         out_specs=[vmem] * 2,
         out_shape=[
-            jax.ShapeDtypeStruct((count, model), bf16),
-            jax.ShapeDtypeStruct(payload, bf16),
+            pltpu.VMEM((count, model), bf16),
+            pltpu.VMEM(payload, bf16),
         ],
         scratch_shapes=[pltpu.VMEM((count, lanes), f32)],
         name="merge_parts",
     )(
         arrived,
-        base_sum,
-        base_peak,
-        base_total,
-        text_embed,
+        pltpu.with_memory_space_constraint(base_sum, pltpu.VMEM),
+        pltpu.with_memory_space_constraint(base_peak, pltpu.VMEM),
+        pltpu.with_memory_space_constraint(base_total, pltpu.VMEM),
+        pltpu.with_memory_space_constraint(text_embed, pltpu.VMEM),
         label_row,
         pltpu.with_memory_space_constraint(out_weight, pltpu.VMEM),
     )
@@ -565,7 +565,7 @@
         peer_copy(other, 0, 3),
         peer_copy(across, 1, 0),
     ]
-    pieces = [own] + [pltpu.with_memory_space_constraint(piece, pltpu.VMEM) for piece in received]
+    pieces = [pltpu.with_memory_space_constraint(piece, pltpu.VMEM) for piece in [own] + received]
     image_grad, text_grad = pl.pallas_call(
         grad_kernel,
         in_specs=[smem, smem, vmem] + [vmem] * peers,

time: 52.1 us -> 49.4 us (0.948)
  Pallas kernels: 21.4 us -> 18.1 us
  local copies, waits for them, and re-layouts: 0.01 us -> 0.65 us
    pallas_call x1, Pallas kernels: 3.31 us -> 1.68 us  [per_device(): pl.pallas_call(merge_body, in_specs=[vmem] * 7, out_specs=[vmem] * 2, out...]
    pallas_call x1, Pallas kernels: 2.47 us -> 1.53 us  [per_device(): pl.pallas_call(grad_kernel, in_specs=[smem, smem, vmem] + [vmem] * peers,...]
    pallas_call x1, Pallas kernels: 6.1 us -> 5.44 us  [per_device(): pl.pallas_call(base_body, in_specs=[anywhere, vmem, anywhere], out_specs=...]
    unnamed x2 -> x7, local copies, waits for them, and re-layouts: 0.01 us -> 0.65 us
    all_to_all x1, waiting for transfers between devices: 2.6 us -> 3.24 us  [per_device(): lax.all_to_all(send, 'dp', split_axis=0, concat_axis=0, tiled=True)]
    ppermute x7, waiting for transfers between devices: 5.08 us -> 4.46 us  [peer_copy(): return lax.ppermute(array, 'loop', pairs)]
  transfers between devices with their start and end apart: 8 -> 8, of which waited for: 3 -> 3; matrix products, arithmetic and copies ran while one was open for 0% -> 1% of each run, Pallas kernels for 12% -> 11%
where the time goes in v1:
time: 49.4 us; the launch traced here: 49.1 us
  starting transfers between devices  20.6 us (42%)
  Pallas kernels  18.1 us (37%)
  waiting for transfers between devices  7.7 us (16%)
  between operations  2 us (4%)
  local copies, waits for them, and re-layouts  0.65 us (1%)
    ppermute x7, starting transfers between devices, peer_copy(): return lax.ppermute(array, 'loop', pairs)  14.1 us
    pallas_call x1, Pallas kernels, per_device(): pl.pallas_call(crop_body, in_specs=[anywhere, vmem, vmem, vmem, vmem, any...  9.5 us
    all_to_all x1, starting transfers between devices, per_device(): lax.all_to_all(send, 'dp', split_axis=0, concat_axis=0, tiled=True)  6.46 us
    pallas_call x1, Pallas kernels, per_device(): pl.pallas_call(base_body, in_specs=[anywhere, vmem, anywhere], out_specs=...  5.44 us
    ppermute x7, waiting for transfers between devices, peer_copy(): return lax.ppermute(array, 'loop', pairs)  4.46 us
    all_to_all x1, waiting for transfers between devices, per_device(): lax.all_to_all(send, 'dp', split_axis=0, concat_axis=0, tiled=True)  3.24 us
    pallas_call x1, Pallas kernels, per_device(): pl.pallas_call(merge_body, in_specs=[vmem] * 7, out_specs=[vmem] * 2, out...  1.68 us
    pallas_call x1, Pallas kernels, per_device(): pl.pallas_call(grad_kernel, in_specs=[smem, smem, vmem] + [vmem] * peers,...  1.53 us
  transfers between devices with their start and end apart: 8, of which 3 were waited for; matrix products, arithmetic and copies ran while one was open for 1% of the time, Pallas kernels for 11%

profile of v1, /device:TPU:0, one launch (start us, length us, event | category | flops | bytes accessed | tf_op | source)
XLA Modules:
  0.0 49.1 jit_solution(18433387659280875108)
XLA Ops:
  0.6 9.5 %crop_partial.1 = bf16[128,1280]{1,0:T(8,128)(2,1)} custom-call(bf16[64,64,1152]{2,1,0:T(8,128)(2,1)} %refs_0_.2, bf16[16,1152]{1,0:T(8,128)(2,1)} %bitcast.10, s32[1,64]{1,0:T(1,128)} %refs_2_.2, s32[1,64]{1,0:T(1,128)} %bitcast.12, s32[1,64]{1,0:T(1,128)} %bitcast.13, bf16[1152,1152]{1,0:T(8,128)(2,1)} %refs_2_.3), custom_call_target="tpu_custom_call" | custom-call | tf_op jit(solution)/shard_map/crop_partial/pallas_call | solution.py:483
  10.1 6.5 %all-to-all-start = ((bf16[16,8,1280]{2,1,0:T(8,128)(2,1)}), bf16[16,8,1280]{2,1,0:T(8,128)(2,1)S(1)}, u32[]{:S(2)}, u32[]{:S(2)}) async-start(bf16[16,8,1280]{2,1,0:T(8,128)(2,1)} %bitcast.9), calls=%async_computation | async-start | bytes 655360 | tf_op jit(solution)/shard_map/all_to_all | solution.py:507
  16.6 0.0 copy-start
  16.6 0.0 copy-start.1
  16.6 0.0 copy-start.2
  16.6 5.4 %base_partial.1 = (f32[32,1152]{1,0:T(8,128)S(1)}, f32[32,128]{1,0:T(8,128)S(1)}, f32[32,128]{1,0:T(8,128)S(1)}) custom-call(bf16[32,32,1152]{2,1,0:T(8,128)(2,1)} %refs_0_.3, bf16[16,1152]{1,0:T(8,128)(2,1)} %bitcast.11, bf16[1152,1152]{1,0:T(8,128)(2,1)} %refs_2_.3), custom_call_target="tpu_custom_call" | custom-call | tf_op jit(solution)/shard_map/base_partial/pallas_call | solution.py:509
  22.1 3.2 %all-to-all-done = bf16[16,8,1280]{2,1,0:T(8,128)(2,1)S(1)} async-done(((bf16[16,8,1280]{2,1,0:T(8,128)(2,1)}), bf16[16,8,1280]{2,1,0:T(8,128)(2,1)S(1)}, u32[]{:S(2)}, u32[]{:S(2)}) %all-to-all-start) | async-done | bytes 327712 | tf_op jit(solution)/shard_map/all_to_all | solution.py:507
  25.3 0.0 copy-done
  25.3 0.0 copy-done.1
  25.3 0.0 copy-done.2
  25.3 1.7 %merge_parts.1 = (bf16[32,1152]{1,0:T(8,128)(2,1)S(1)}, bf16[592,128]{1,0:T(8,128)(2,1)S(1)}) custom-call(bf16[128,1280]{1,0:T(8,128)(2,1)S(1)} %bitcast.6, f32[32,1152]{1,0:T(8,128)S(1)} %get-tuple-element.10.refs_1_, f32[32,128]{1,0:T(8,128)S(1)} %get-tuple-element.11.refs_2_, f32[32,128]{1,0:T(8,128)S(1)} %get-tuple-element.12.refs_3_, ...), custom_call_target="tpu_custom_call" | custom-call | tf_op jit(solution)/shard_map/merge_parts/pallas_call | solution.py:528
  27.0 3.3 %collective-permute-start.3 = (bf16[592,128]{1,0:T(8,128)(2,1)S(1)}, bf16[592,128]{1,0:T(8,128)(2,1)S(1)}, u32[]{:S(2)}, u32[]{:S(2)}) collective-permute-start(bf16[592,128]{1,0:T(8,128)(2,1)S(1)} %get-tuple-element.14.refs_0_), channel_id=1, source_target_pairs={{0,2},{1,3},{2,0},{3,1},{4,6},{5,7},{6,4},{7,5},{8,10},{9,11},{10,... | collective-permute-start | bytes 454664 | tf_op jit(solution)/shard_map/ppermute | solution.py:553
  30.3 2.7 %collective-permute-start = (bf16[592,128]{1,0:T(8,128)(2,1)S(1)}, bf16[592,128]{1,0:T(8,128)(2,1)S(1)}, u32[]{:S(2)}, u32[]{:S(2)}) collective-permute-start(bf16[592,128]{1,0:T(8,128)(2,1)S(1)} %get-tuple-element.14.refs_0_), channel_id=1, source_target_pairs={{0,4},{1,5},{2,6},{3,7},{4,0},{5,1},{6,2},{7,3},{8,12},{9,13},{10,... | collective-permute-start | bytes 454664 | tf_op jit(solution)/shard_map/ppermute | solution.py:553
  33.0 1.1 %collective-permute-start.2 = (bf16[592,128]{1,0:T(8,128)(2,1)S(1)}, bf16[592,128]{1,0:T(8,128)(2,1)S(1)}, u32[]{:S(2)}, u32[]{:S(2)}) collective-permute-start(bf16[592,128]{1,0:T(8,128)(2,1)S(1)} %get-tuple-element.14.refs_0_), channel_id=1, source_target_pairs={{0,3},{1,0},{2,1},{3,2},{4,7},{5,4},{6,5},{7,6},{8,11},{9,8},{10,9... | collective-permute-start | bytes 454664 | tf_op jit(solution)/shard_map/ppermute | solution.py:553
  34.1 1.0 %collective-permute-start.1 = (bf16[592,128]{1,0:T(8,128)(2,1)S(1)}, bf16[592,128]{1,0:T(8,128)(2,1)S(1)}, u32[]{:S(2)}, u32[]{:S(2)}) collective-permute-start(bf16[592,128]{1,0:T(8,128)(2,1)S(1)} %get-tuple-element.14.refs_0_), channel_id=1, source_target_pairs={{0,1},{1,2},{2,3},{3,0},{4,5},{5,6},{6,7},{7,4},{8,9},{9,10},{10,1... | collective-permute-start | bytes 454664 | tf_op jit(solution)/shard_map/ppermute | solution.py:553
  35.1 0.0 collective-permute-done.3.refs_4_
  35.1 2.1 %collective-permute-start.6 = (bf16[592,128]{1,0:T(8,128)(2,1)S(1)}, bf16[592,128]{1,0:T(8,128)(2,1)S(1)}, u32[]{:S(2)}, u32[]{:S(2)}) collective-permute-start(bf16[592,128]{1,0:T(8,128)(2,1)S(1)} %collective-permute-done.3.refs_4_), channel_id=1, source_target_pairs={{0,4},{1,5},{2,6},{3,7},{4,0},{5,1},{6,2},{7,3},{8,12},{9,13},{10,... | collective-permute-start | bytes 454664 | tf_op jit(solution)/shard_map/ppermute | solution.py:553
  37.2 0.0 collective-permute-done.refs_1_
  37.2 4.0 %collective-permute-start.5 = (bf16[592,128]{1,0:T(8,128)(2,1)S(1)}, bf16[592,128]{1,0:T(8,128)(2,1)S(1)}, u32[]{:S(2)}, u32[]{:S(2)}) collective-permute-start(bf16[592,128]{1,0:T(8,128)(2,1)S(1)} %collective-permute-done.refs_1_), channel_id=1, source_target_pairs={{0,3},{1,0},{2,1},{3,2},{4,7},{5,4},{6,5},{7,6},{8,11},{9,8},{10,9... | collective-permute-start | bytes 454664 | tf_op jit(solution)/shard_map/ppermute | solution.py:553
  41.2 0.0 collective-permute-start.4
  42.5 0.6 %copy.15 = bf16[32,1152]{1,0:T(8,128)(2,1)} copy(bf16[32,1152]{1,0:T(8,128)(2,1)S(1)} %get-tuple-element.17) | data formatting | bytes 147456
  43.1 0.0 collective-permute-done.2.refs_3_
  43.1 0.0 collective-permute-done.1.refs_2_
  43.1 0.0 collective-permute-done.6.refs_7_
  43.1 0.8 %collective-permute-done.5.refs_6_ = bf16[592,128]{1,0:T(8,128)(2,1)S(1)} collective-permute-done((bf16[592,128]{1,0:T(8,128)(2,1)S(1)}, bf16[592,128]{1,0:T(8,128)(2,1)S(1)}, u32[]{:S(2)}, u32[]{:S(2)}) %collective-permute-start.5) | collective-permute-done | bytes 151584 | tf_op jit(solution)/shard_map/ppermute | solution.py:553
  43.9 3.7 %collective-permute-done.4.refs_5_ = bf16[592,128]{1,0:T(8,128)(2,1)S(1)} collective-permute-done((bf16[592,128]{1,0:T(8,128)(2,1)S(1)}, bf16[592,128]{1,0:T(8,128)(2,1)S(1)}, u32[]{:S(2)}, u32[]{:S(2)}) %collective-permute-start.4) | collective-permute-done | bytes 151584 | tf_op jit(solution)/shard_map/ppermute | solution.py:553
  47.6 1.5 %loss_grads.1 = (f32[32,1152]{1,0:T(8,128)}, f32[32,1152]{1,0:T(8,128)}) custom-call(f32[1]{0:T(128)S(6)} %copy.16.scale_ref, f32[1]{0:T(128)S(6)} %copy.17.bias_ref, s32[1,32]{1,0:T(1,128)S(1)} %bitcast.8, bf16[592,128]{1,0:T(8,128)(2,1)S(1)} %get-tuple-element.14.refs_0_, bf16[592,128]{1,0:T(8,128)(2,1)S(1)} %collective-permute-done.refs_1_, ...), custom_call_target="tpu_custom_call" | custom-call | tf_op jit(solution)/shard_map/loss_grads/pallas_call | solution.py:569
Async XLA Ops:
  10.1 15.2 %all-to-all-start = ((bf16[16,8,1280]{2,1,0:T(8,128)(2,1)}), bf16[16,8,1280]{2,1,0:T(8,128)(2,1)S(1)}, u32[]{:S(2)}, u32[]{:S(2)}) async-start(bf16[16,8,1280]{2,1,0:T(8,128)(2,1)} %bitcast.9), calls=%async_computation | async-start | bytes 655360 | tf_op jit(solution)/shard_map/all_to_all | solution.py:507
  16.6 8.7 %copy-start = (bf16[1152,1152]{1,0:T(8,128)(2,1)S(1)}, bf16[1152,1152]{1,0:T(8,128)(2,1)}, u32[]{:S(2)}) copy-start(bf16[1152,1152]{1,0:T(8,128)(2,1)} %refs_6_.1) | copy-start | bytes 7962628
  16.6 8.7 %copy-start.1 = (bf16[32,1152]{1,0:T(8,128)(2,1)S(1)}, bf16[32,1152]{1,0:T(8,128)(2,1)}, u32[]{:S(2)}) copy-start(bf16[32,1152]{1,0:T(8,128)(2,1)} %refs_4_.1) | copy-start | bytes 221188
  16.6 8.7 %copy-start.2 = (s32[32]{0:T(128)S(1)}, s32[32]{0:T(128)}, u32[]{:S(2)}) copy-start(s32[32]{0:T(128)} %param.21) | copy-start | bytes 388
  27.0 8.0 %collective-permute-start.3 = (bf16[592,128]{1,0:T(8,128)(2,1)S(1)}, bf16[592,128]{1,0:T(8,128)(2,1)S(1)}, u32[]{:S(2)}, u32[]{:S(2)}) collective-permute-start(bf16[592,128]{1,0:T(8,128)(2,1)S(1)} %get-tuple-element.14.refs_0_), channel_id=1, source_target_pairs={{0,2},{1,3},{2,0},{3,1},{4,6},{5,7},{6,4},{7,5},{8,10},{9,11},{10,... | collective-permute-start | bytes 454664 | tf_op jit(solution)/shard_map/ppermute | solution.py:553
  30.3 6.9 %collective-permute-start = (bf16[592,128]{1,0:T(8,128)(2,1)S(1)}, bf16[592,128]{1,0:T(8,128)(2,1)S(1)}, u32[]{:S(2)}, u32[]{:S(2)}) collective-permute-start(bf16[592,128]{1,0:T(8,128)(2,1)S(1)} %get-tuple-element.14.refs_0_), channel_id=1, source_target_pairs={{0,4},{1,5},{2,6},{3,7},{4,0},{5,1},{6,2},{7,3},{8,12},{9,13},{10,... | collective-permute-start | bytes 454664 | tf_op jit(solution)/shard_map/ppermute | solution.py:553
  33.0 10.1 %collective-permute-start.2 = (bf16[592,128]{1,0:T(8,128)(2,1)S(1)}, bf16[592,128]{1,0:T(8,128)(2,1)S(1)}, u32[]{:S(2)}, u32[]{:S(2)}) collective-permute-start(bf16[592,128]{1,0:T(8,128)(2,1)S(1)} %get-tuple-element.14.refs_0_), channel_id=1, source_target_pairs={{0,3},{1,0},{2,1},{3,2},{4,7},{5,4},{6,5},{7,6},{8,11},{9,8},{10,9... | collective-permute-start | bytes 454664 | tf_op jit(solution)/shard_map/ppermute | solution.py:553
  34.1 9.0 %collective-permute-start.1 = (bf16[592,128]{1,0:T(8,128)(2,1)S(1)}, bf16[592,128]{1,0:T(8,128)(2,1)S(1)}, u32[]{:S(2)}, u32[]{:S(2)}) collective-permute-start(bf16[592,128]{1,0:T(8,128)(2,1)S(1)} %get-tuple-element.14.refs_0_), channel_id=1, source_target_pairs={{0,1},{1,2},{2,3},{3,0},{4,5},{5,6},{6,7},{7,4},{8,9},{9,10},{10,1... | collective-permute-start | bytes 454664 | tf_op jit(solution)/shard_map/ppermute | solution.py:553
  35.1 8.1 %collective-permute-start.6 = (bf16[592,128]{1,0:T(8,128)(2,1)S(1)}, bf16[592,128]{1,0:T(8,128)(2,1)S(1)}, u32[]{:S(2)}, u32[]{:S(2)}) collective-permute-start(bf16[592,128]{1,0:T(8,128)(2,1)S(1)} %collective-permute-done.3.refs_4_), channel_id=1, source_target_pairs={{0,4},{1,5},{2,6},{3,7},{4,0},{5,1},{6,2},{7,3},{8,12},{9,13},{10,... | collective-permute-start | bytes 454664 | tf_op jit(solution)/shard_map/ppermute | solution.py:553
  37.2 6.7 %collective-permute-start.5 = (bf16[592,128]{1,0:T(8,128)(2,1)S(1)}, bf16[592,128]{1,0:T(8,128)(2,1)S(1)}, u32[]{:S(2)}, u32[]{:S(2)}) collective-permute-start(bf16[592,128]{1,0:T(8,128)(2,1)S(1)} %collective-permute-done.refs_1_), channel_id=1, source_target_pairs={{0,3},{1,0},{2,1},{3,2},{4,7},{5,4},{6,5},{7,6},{8,11},{9,8},{10,9... | collective-permute-start | bytes 454664 | tf_op jit(solution)/shard_map/ppermute | solution.py:553
  41.2 6.4 %collective-permute-start.4 = (bf16[592,128]{1,0:T(8,128)(2,1)S(1)}, bf16[592,128]{1,0:T(8,128)(2,1)S(1)}, u32[]{:S(2)}, u32[]{:S(2)}) collective-permute-start(bf16[592,128]{1,0:T(8,128)(2,1)S(1)} %collective-permute-done.refs_1_), channel_id=1, source_target_pairs={{0,1},{1,2},{2,3},{3,0},{4,5},{5,6},{6,7},{7,4},{8,9},{9,10},{10,1... | collective-permute-start | bytes 454664 | tf_op jit(solution)/shard_map/ppermute | solution.py:553

commit v2 on v1

--- a/solution.py
+++ b/solution.py
@@ -78,15 +78,22 @@
         ).astype(bf16)
 
 
-def project_tile(rows_ref, value_ref, stride, low, high, head_dim, units):
+def project_tile(rows_ref, value_ref, stride, low, high, head_dim, units, begin=0, end=None):
     span = sublanes // units * head_dim
     first = low // span
     last = (high - 1) // span
+    end = stride if end is None else end
     stacked = jnp.dot(
-        rows_ref[first * stride : (last + 1) * stride, :],
+        jnp.concatenate(
+            [
+                rows_ref[tile * stride + begin : tile * stride + end, :]
+                for tile in range(first, last + 1)
+            ],
+            axis=0,
+        ),
         value_ref[:, low:high],
         preferred_element_type=f32,
-    ).reshape(last + 1 - first, stride // sublanes, sublanes, high - low)
+    ).reshape(last + 1 - first, (end - begin) // sublanes, sublanes, high - low)
     shape = (1, sublanes, high - low)
     kind = iota(shape, 1) // units
     column = iota(shape, 2) + low - kind * head_dim
@@ -96,7 +103,7 @@
     if units < sublanes:
         owner = (column >= 0) & (column % span < head_dim)
         total = jnp.where(owner, total, 0.0)
-    return total.reshape(stride, high - low)
+    return total.reshape(end - begin, high - low)
 
 
 def project_heads(rows_ref, value_ref, stride, model, head_dim, units, finish):
@@ -128,6 +135,7 @@
     meta_ref,
     limit_ref,
     member_ref,
+    summed_ref,
     value_ref,
     token_sem,
     value_sem,
@@ -149,10 +157,11 @@
         where = pl.ds(step * per_step, per_step)
         return pltpu.make_async_copy(token_hbm.at[where], token_ref.at[where], token_sem.at[step])
 
+    value_copy = pltpu.make_async_copy(value_hbm, value_ref, value_sem)
     for step in range(blocks):
+        if step == blocks // 2:
+            value_copy.start()
         token_copy(step).start()
-    value_copy = pltpu.make_async_copy(value_hbm, value_ref, value_sem)
-    value_copy.start()
     expand = (rows, crops)
     owner_of = iota(expand, 0) // sublanes * units + iota(expand, 0) % units
     chosen = owner_of == iota(expand, 1)
@@ -232,20 +241,33 @@
         following = scores_of(step + 1)
         return following, weigh(step, scores)
 
-    scores, weights = lax.fori_loop(1, blocks - 1, advance, (following, weights))
+    half = rows // 2
+    columns = [(low, min(low + col_tile, model)) for low in range(0, model, col_tile)]
+
+    def project(tiles, begin, end):
+        for low, high in tiles:
+            summed_ref[begin:end, low:high] = project_tile(
+                rows_ref, value_ref, rows, low, high, head_dim, units, begin, end
+            ).astype(bf16)
+
+    middle = blocks // 2 + 1
+    scores, weights = lax.fori_loop(1, middle, advance, (following, weights))
+    value_copy.wait()
+    spread = blocks - 1 - middle
+    for step in range(middle, blocks - 1):
+        scores, weights = advance(step, (scores, weights))
+        project(columns[step - middle :: spread + 1], 0, half)
     mix(blocks - 2, weights)
-    mix(blocks - 1, weigh(blocks - 1, scores))
+    weights = weigh(blocks - 1, scores)
+    project(columns[spread :: spread + 1], 0, half)
+    mix(blocks - 1, weights)
+    project(columns, half, rows)
     send_ref[:, model:] = jnp.dot(
         member_ref[...], meta_ref[...].astype(bf16), preferred_element_type=f32
     ).astype(bf16)
-    value_copy.wait()
-
-    def finish(low, high, summed):
-        send_ref[:, low:high] = jnp.dot(
-            member_ref[...], summed.astype(bf16), preferred_element_type=f32
-        ).astype(bf16)
-
-    project_heads(rows_ref, value_ref, rows, model, head_dim, units, finish)
+    send_ref[:, :model] = jnp.dot(
+        member_ref[...], summed_ref[...], preferred_element_type=f32
+    ).astype(bf16)
 
 
 def base_kernel(
@@ -490,6 +512,7 @@
             pltpu.VMEM((rows, lanes), f32),
             pltpu.VMEM((rows, lanes), jnp.int32),
             pltpu.VMEM((slots, rows), bf16),
+            pltpu.VMEM((rows, model), bf16),
             pltpu.VMEM((model, model), bf16),
             pltpu.SemaphoreType.DMA((blocks,)),
             pltpu.SemaphoreType.DMA,

time: 49.4 us -> 49 us (level)
  no operation moved by 1% of the time
where the time goes in v2:
time: 49 us; the launch traced here: 48.7 us
  starting transfers between devices  20.6 us (42%)
  Pallas kernels  17.8 us (36%)
  waiting for transfers between devices  7.69 us (16%)
  between operations  2 us (4%)
  local copies, waits for them, and re-layouts  0.65 us (1%)
    ppermute x7, starting transfers between devices, peer_copy(): return lax.ppermute(array, 'loop', pairs)  14.1 us
    pallas_call x1, Pallas kernels, per_device(): pl.pallas_call(crop_body, in_specs=[anywhere, vmem, vmem, vmem, vmem, any...  9.1 us
    all_to_all x1, starting transfers between devices, per_device(): lax.all_to_all(send, 'dp', split_axis=0, concat_axis=0, tiled=True)  6.47 us
    pallas_call x1, Pallas kernels, per_device(): pl.pallas_call(base_body, in_specs=[anywhere, vmem, anywhere], out_specs=...  5.45 us
    ppermute x7, waiting for transfers between devices, peer_copy(): return lax.ppermute(array, 'loop', pairs)  4.46 us
    all_to_all x1, waiting for transfers between devices, per_device(): lax.all_to_all(send, 'dp', split_axis=0, concat_axis=0, tiled=True)  3.23 us
    pallas_call x1, Pallas kernels, per_device(): pl.pallas_call(merge_body, in_specs=[vmem] * 7, out_specs=[vmem] * 2, out...  1.68 us
    pallas_call x1, Pallas kernels, per_device(): pl.pallas_call(grad_kernel, in_specs=[smem, smem, vmem] + [vmem] * peers,...  1.54 us
  transfers between devices with their start and end apart: 8, of which 3 were waited for; matrix products, arithmetic and copies ran while one was open for 1% of the time, Pallas kernels for 11%

profile of v2, /device:TPU:0, one launch (start us, length us, event | category | flops | bytes accessed | tf_op | source)
XLA Modules:
  0.0 48.7 jit_solution(498947804674328132)
XLA Ops:
  0.6 9.1 %crop_partial.1 = bf16[128,1280]{1,0:T(8,128)(2,1)} custom-call(bf16[64,64,1152]{2,1,0:T(8,128)(2,1)} %refs_0_.2, bf16[16,1152]{1,0:T(8,128)(2,1)} %bitcast.10, s32[1,64]{1,0:T(1,128)} %refs_2_.2, s32[1,64]{1,0:T(1,128)} %bitcast.12, s32[1,64]{1,0:T(1,128)} %bitcast.13, bf16[1152,1152]{1,0:T(8,128)(2,1)} %refs_2_.3), custom_call_target="tpu_custom_call" | custom-call | tf_op jit(solution)/shard_map/crop_partial/pallas_call | solution.py:505
  9.7 6.5 %all-to-all-start = ((bf16[16,8,1280]{2,1,0:T(8,128)(2,1)}), bf16[16,8,1280]{2,1,0:T(8,128)(2,1)S(1)}, u32[]{:S(2)}, u32[]{:S(2)}) async-start(bf16[16,8,1280]{2,1,0:T(8,128)(2,1)} %bitcast.9), calls=%async_computation | async-start | bytes 655360 | tf_op jit(solution)/shard_map/all_to_all | solution.py:530
  16.2 0.0 copy-start
  16.2 0.0 copy-start.1
  16.2 0.0 copy-start.2
  16.3 5.4 %base_partial.1 = (f32[32,1152]{1,0:T(8,128)S(1)}, f32[32,128]{1,0:T(8,128)S(1)}, f32[32,128]{1,0:T(8,128)S(1)}) custom-call(bf16[32,32,1152]{2,1,0:T(8,128)(2,1)} %refs_0_.3, bf16[16,1152]{1,0:T(8,128)(2,1)} %bitcast.11, bf16[1152,1152]{1,0:T(8,128)(2,1)} %refs_2_.3), custom_call_target="tpu_custom_call" | custom-call | tf_op jit(solution)/shard_map/base_partial/pallas_call | solution.py:532
  21.7 3.2 %all-to-all-done = bf16[16,8,1280]{2,1,0:T(8,128)(2,1)S(1)} async-done(((bf16[16,8,1280]{2,1,0:T(8,128)(2,1)}), bf16[16,8,1280]{2,1,0:T(8,128)(2,1)S(1)}, u32[]{:S(2)}, u32[]{:S(2)}) %all-to-all-start) | async-done | bytes 327712 | tf_op jit(solution)/shard_map/all_to_all | solution.py:530
  24.9 0.0 copy-done
  24.9 0.0 copy-done.1
  24.9 0.0 copy-done.2
  25.0 1.7 %merge_parts.1 = (bf16[32,1152]{1,0:T(8,128)(2,1)S(1)}, bf16[592,128]{1,0:T(8,128)(2,1)S(1)}) custom-call(bf16[128,1280]{1,0:T(8,128)(2,1)S(1)} %bitcast.6, f32[32,1152]{1,0:T(8,128)S(1)} %get-tuple-element.10.refs_1_, f32[32,128]{1,0:T(8,128)S(1)} %get-tuple-element.11.refs_2_, f32[32,128]{1,0:T(8,128)S(1)} %get-tuple-element.12.refs_3_, ...), custom_call_target="tpu_custom_call" | custom-call | tf_op jit(solution)/shard_map/merge_parts/pallas_call | solution.py:551
  26.6 3.3 %collective-permute-start.3 = (bf16[592,128]{1,0:T(8,128)(2,1)S(1)}, bf16[592,128]{1,0:T(8,128)(2,1)S(1)}, u32[]{:S(2)}, u32[]{:S(2)}) collective-permute-start(bf16[592,128]{1,0:T(8,128)(2,1)S(1)} %get-tuple-element.14.refs_0_), channel_id=1, source_target_pairs={{0,2},{1,3},{2,0},{3,1},{4,6},{5,7},{6,4},{7,5},{8,10},{9,11},{10,... | collective-permute-start | bytes 454664 | tf_op jit(solution)/shard_map/ppermute | solution.py:576
  29.9 2.7 %collective-permute-start = (bf16[592,128]{1,0:T(8,128)(2,1)S(1)}, bf16[592,128]{1,0:T(8,128)(2,1)S(1)}, u32[]{:S(2)}, u32[]{:S(2)}) collective-permute-start(bf16[592,128]{1,0:T(8,128)(2,1)S(1)} %get-tuple-element.14.refs_0_), channel_id=1, source_target_pairs={{0,4},{1,5},{2,6},{3,7},{4,0},{5,1},{6,2},{7,3},{8,12},{9,13},{10,... | collective-permute-start | bytes 454664 | tf_op jit(solution)/shard_map/ppermute | solution.py:576
  32.6 1.1 %collective-permute-start.2 = (bf16[592,128]{1,0:T(8,128)(2,1)S(1)}, bf16[592,128]{1,0:T(8,128)(2,1)S(1)}, u32[]{:S(2)}, u32[]{:S(2)}) collective-permute-start(bf16[592,128]{1,0:T(8,128)(2,1)S(1)} %get-tuple-element.14.refs_0_), channel_id=1, source_target_pairs={{0,3},{1,0},{2,1},{3,2},{4,7},{5,4},{6,5},{7,6},{8,11},{9,8},{10,9... | collective-permute-start | bytes 454664 | tf_op jit(solution)/shard_map/ppermute | solution.py:576
  33.7 1.0 %collective-permute-start.1 = (bf16[592,128]{1,0:T(8,128)(2,1)S(1)}, bf16[592,128]{1,0:T(8,128)(2,1)S(1)}, u32[]{:S(2)}, u32[]{:S(2)}) collective-permute-start(bf16[592,128]{1,0:T(8,128)(2,1)S(1)} %get-tuple-element.14.refs_0_), channel_id=1, source_target_pairs={{0,1},{1,2},{2,3},{3,0},{4,5},{5,6},{6,7},{7,4},{8,9},{9,10},{10,1... | collective-permute-start | bytes 454664 | tf_op jit(solution)/shard_map/ppermute | solution.py:576
  34.7 0.0 collective-permute-done.3.refs_4_
  34.7 2.1 %collective-permute-start.6 = (bf16[592,128]{1,0:T(8,128)(2,1)S(1)}, bf16[592,128]{1,0:T(8,128)(2,1)S(1)}, u32[]{:S(2)}, u32[]{:S(2)}) collective-permute-start(bf16[592,128]{1,0:T(8,128)(2,1)S(1)} %collective-permute-done.3.refs_4_), channel_id=1, source_target_pairs={{0,4},{1,5},{2,6},{3,7},{4,0},{5,1},{6,2},{7,3},{8,12},{9,13},{10,... | collective-permute-start | bytes 454664 | tf_op jit(solution)/shard_map/ppermute | solution.py:576
  36.8 0.0 collective-permute-done.refs_1_
  36.8 4.0 %collective-permute-start.5 = (bf16[592,128]{1,0:T(8,128)(2,1)S(1)}, bf16[592,128]{1,0:T(8,128)(2,1)S(1)}, u32[]{:S(2)}, u32[]{:S(2)}) collective-permute-start(bf16[592,128]{1,0:T(8,128)(2,1)S(1)} %collective-permute-done.refs_1_), channel_id=1, source_target_pairs={{0,3},{1,0},{2,1},{3,2},{4,7},{5,4},{6,5},{7,6},{8,11},{9,8},{10,9... | collective-permute-start | bytes 454664 | tf_op jit(solution)/shard_map/ppermute | solution.py:576
  40.8 0.0 collective-permute-start.4
  42.1 0.6 %copy.15 = bf16[32,1152]{1,0:T(8,128)(2,1)} copy(bf16[32,1152]{1,0:T(8,128)(2,1)S(1)} %get-tuple-element.17) | data formatting | bytes 147456
  42.7 0.0 collective-permute-done.2.refs_3_
  42.7 0.0 collective-permute-done.1.refs_2_
  42.7 0.0 collective-permute-done.6.refs_7_
  42.7 0.8 %collective-permute-done.5.refs_6_ = bf16[592,128]{1,0:T(8,128)(2,1)S(1)} collective-permute-done((bf16[592,128]{1,0:T(8,128)(2,1)S(1)}, bf16[592,128]{1,0:T(8,128)(2,1)S(1)}, u32[]{:S(2)}, u32[]{:S(2)}) %collective-permute-start.5) | collective-permute-done | bytes 151584 | tf_op jit(solution)/shard_map/ppermute | solution.py:576
  43.5 3.7 %collective-permute-done.4.refs_5_ = bf16[592,128]{1,0:T(8,128)(2,1)S(1)} collective-permute-done((bf16[592,128]{1,0:T(8,128)(2,1)S(1)}, bf16[592,128]{1,0:T(8,128)(2,1)S(1)}, u32[]{:S(2)}, u32[]{:S(2)}) %collective-permute-start.4) | collective-permute-done | bytes 151584 | tf_op jit(solution)/shard_map/ppermute | solution.py:576
  47.2 1.5 %loss_grads.1 = (f32[32,1152]{1,0:T(8,128)}, f32[32,1152]{1,0:T(8,128)}) custom-call(f32[1]{0:T(128)S(6)} %copy.16.scale_ref, f32[1]{0:T(128)S(6)} %copy.17.bias_ref, s32[1,32]{1,0:T(1,128)S(1)} %bitcast.8, bf16[592,128]{1,0:T(8,128)(2,1)S(1)} %get-tuple-element.14.refs_0_, bf16[592,128]{1,0:T(8,128)(2,1)S(1)} %collective-permute-done.refs_1_, ...), custom_call_target="tpu_custom_call" | custom-call | tf_op jit(solution)/shard_map/loss_grads/pallas_call | solution.py:592
Async XLA Ops:
  9.7 15.2 %all-to-all-start = ((bf16[16,8,1280]{2,1,0:T(8,128)(2,1)}), bf16[16,8,1280]{2,1,0:T(8,128)(2,1)S(1)}, u32[]{:S(2)}, u32[]{:S(2)}) async-start(bf16[16,8,1280]{2,1,0:T(8,128)(2,1)} %bitcast.9), calls=%async_computation | async-start | bytes 655360 | tf_op jit(solution)/shard_map/all_to_all | solution.py:530
  16.2 8.7 %copy-start = (bf16[1152,1152]{1,0:T(8,128)(2,1)S(1)}, bf16[1152,1152]{1,0:T(8,128)(2,1)}, u32[]{:S(2)}) copy-start(bf16[1152,1152]{1,0:T(8,128)(2,1)} %refs_6_.1) | copy-start | bytes 7962628
  16.2 8.7 %copy-start.1 = (bf16[32,1152]{1,0:T(8,128)(2,1)S(1)}, bf16[32,1152]{1,0:T(8,128)(2,1)}, u32[]{:S(2)}) copy-start(bf16[32,1152]{1,0:T(8,128)(2,1)} %refs_4_.1) | copy-start | bytes 221188
  16.2 8.7 %copy-start.2 = (s32[32]{0:T(128)S(1)}, s32[32]{0:T(128)}, u32[]{:S(2)}) copy-start(s32[32]{0:T(128)} %param.21) | copy-start | bytes 388
  26.6 8.0 %collective-permute-start.3 = (bf16[592,128]{1,0:T(8,128)(2,1)S(1)}, bf16[592,128]{1,0:T(8,128)(2,1)S(1)}, u32[]{:S(2)}, u32[]{:S(2)}) collective-permute-start(bf16[592,128]{1,0:T(8,128)(2,1)S(1)} %get-tuple-element.14.refs_0_), channel_id=1, source_target_pairs={{0,2},{1,3},{2,0},{3,1},{4,6},{5,7},{6,4},{7,5},{8,10},{9,11},{10,... | collective-permute-start | bytes 454664 | tf_op jit(solution)/shard_map/ppermute | solution.py:576
  29.9 6.8 %collective-permute-start = (bf16[592,128]{1,0:T(8,128)(2,1)S(1)}, bf16[592,128]{1,0:T(8,128)(2,1)S(1)}, u32[]{:S(2)}, u32[]{:S(2)}) collective-permute-start(bf16[592,128]{1,0:T(8,128)(2,1)S(1)} %get-tuple-element.14.refs_0_), channel_id=1, source_target_pairs={{0,4},{1,5},{2,6},{3,7},{4,0},{5,1},{6,2},{7,3},{8,12},{9,13},{10,... | collective-permute-start | bytes 454664 | tf_op jit(solution)/shard_map/ppermute | solution.py:576
  32.6 10.1 %collective-permute-start.2 = (bf16[592,128]{1,0:T(8,128)(2,1)S(1)}, bf16[592,128]{1,0:T(8,128)(2,1)S(1)}, u32[]{:S(2)}, u32[]{:S(2)}) collective-permute-start(bf16[592,128]{1,0:T(8,128)(2,1)S(1)} %get-tuple-element.14.refs_0_), channel_id=1, source_target_pairs={{0,3},{1,0},{2,1},{3,2},{4,7},{5,4},{6,5},{7,6},{8,11},{9,8},{10,9... | collective-permute-start | bytes 454664 | tf_op jit(solution)/shard_map/ppermute | solution.py:576
  33.7 9.0 %collective-permute-start.1 = (bf16[592,128]{1,0:T(8,128)(2,1)S(1)}, bf16[592,128]{1,0:T(8,128)(2,1)S(1)}, u32[]{:S(2)}, u32[]{:S(2)}) collective-permute-start(bf16[592,128]{1,0:T(8,128)(2,1)S(1)} %get-tuple-element.14.refs_0_), channel_id=1, source_target_pairs={{0,1},{1,2},{2,3},{3,0},{4,5},{5,6},{6,7},{7,4},{8,9},{9,10},{10,1... | collective-permute-start | bytes 454664 | tf_op jit(solution)/shard_map/ppermute | solution.py:576
  34.7 8.1 %collective-permute-start.6 = (bf16[592,128]{1,0:T(8,128)(2,1)S(1)}, bf16[592,128]{1,0:T(8,128)(2,1)S(1)}, u32[]{:S(2)}, u32[]{:S(2)}) collective-permute-start(bf16[592,128]{1,0:T(8,128)(2,1)S(1)} %collective-permute-done.3.refs_4_), channel_id=1, source_target_pairs={{0,4},{1,5},{2,6},{3,7},{4,0},{5,1},{6,2},{7,3},{8,12},{9,13},{10,... | collective-permute-start | bytes 454664 | tf_op jit(solution)/shard_map/ppermute | solution.py:576
  36.8 6.7 %collective-permute-start.5 = (bf16[592,128]{1,0:T(8,128)(2,1)S(1)}, bf16[592,128]{1,0:T(8,128)(2,1)S(1)}, u32[]{:S(2)}, u32[]{:S(2)}) collective-permute-start(bf16[592,128]{1,0:T(8,128)(2,1)S(1)} %collective-permute-done.refs_1_), channel_id=1, source_target_pairs={{0,3},{1,0},{2,1},{3,2},{4,7},{5,4},{6,5},{7,6},{8,11},{9,8},{10,9... | collective-permute-start | bytes 454664 | tf_op jit(solution)/shard_map/ppermute | solution.py:576
  40.8 6.4 %collective-permute-start.4 = (bf16[592,128]{1,0:T(8,128)(2,1)S(1)}, bf16[592,128]{1,0:T(8,128)(2,1)S(1)}, u32[]{:S(2)}, u32[]{:S(2)}) collective-permute-start(bf16[592,128]{1,0:T(8,128)(2,1)S(1)} %collective-permute-done.refs_1_), channel_id=1, source_target_pairs={{0,1},{1,2},{2,3},{3,0},{4,5},{5,6},{6,7},{7,4},{8,9},{9,10},{10,1... | collective-permute-start | bytes 454664 | tf_op jit(solution)/shard_map/ppermute | solution.py:576
